TPU v7x, 32 devices: a whole 2x2x4 slice. The times are simulated.
32 devices in a mesh: dp: 4 (over y, core), expert: 8 (over z, x).
Axes of the slice: x: 2, y: 2, z: 4, core: 2. Of those that a mesh axis runs over, the one named last changes fastest.
Arguments:
- tokens: bfloat16 [8, 16, 4096], P('expert', None, 'dp'), may hold values from -6 to 6
- routes: int32 [8, 16, 8], P('expert'), may hold values from 0 to 7, all different within a row; in each aligned block of 16 rows (0 to 15, 16 to 31, ..., all dimensions but the last counted through in order) at most 16 rows name the same one
- gates: float32 [8, 16, 8], P('expert'), may hold values from 0.05 to 0.3
- plan: int32 [8], replicated, may hold values from 0 to 7, each once
- proj_weight: bfloat16 [8, 2, 4096, 768], P('expert', None, 'dp'), may hold values from -0.09375 to 0.09375
- proj_grad: bfloat16 [8, 2, 4096, 768], P('expert', None, 'dp'), may hold values from -6 to 6
- first_moment: float32 [8, 2, 4096, 768], P('expert', None, 'dp'), may hold values from -1.8 to 1.8
- second_moment: float32 [8, 2, 4096, 768], P('expert', None, 'dp'), may hold values from 0.01 to 0.1
- down_weight: bfloat16 [8, 768, 4096], P('expert', None, 'dp'), may hold values from -0.21875 to 0.21875
Outputs:
- out_tokens: bfloat16 [8, 16, 4096], P('expert', None, 'dp')
- new_proj: bfloat16 [8, 2, 4096, 768], P('expert', None, 'dp')
- new_down: bfloat16 [8, 768, 4096], P('expert', None, 'dp')
Inputs may be any that keep to these rules, and one draw needn't show every extreme that they name: `routes`: each token names 8 different experts; within one group no expert is named by more than 16 tokens, and in some group some expert is named by exactly 16. Expert x moves to the owner plan[x]; every owner receives exactly one expert.
All inputs are finite; a program needn't handle non-finite values.
Results may differ from a plain program's by a relative error of at most 0.024.
Values may be sent and summed in bfloat16 or wider, within the bound.
A program may use at most 64 MiB of HBM per device.

v0:
```python
import jax
import jax.numpy as jnp
from jax import lax
from jax.sharding import PartitionSpec as P

learning_rate = 0.01
beta_first = 0.9
beta_second = 0.999
adam_epsilon = 1e-08
bias_first = 1.0 - 0.9**10
bias_second = 1.0 - 0.999**10


def adam_update(weights, grads, first_moment, second_moment):
    grad_float = grads.astype(jnp.float32)
    first_new = beta_first * first_moment + (1.0 - beta_first) * grad_float
    second_new = beta_second * second_moment + (1.0 - beta_second) * grad_float * grad_float
    adam_step = first_new / bias_first / (jnp.sqrt(second_new / bias_second) + adam_epsilon)
    return (weights.astype(jnp.float32) - learning_rate * adam_step).astype(jnp.bfloat16)


def expert_rows(slots, proj_local, down_local):
    width = proj_local.shape[2]
    joined = jnp.concatenate([proj_local[0], proj_local[1]], axis=1)
    summed = lax.psum_scatter(
        jnp.dot(slots, joined, preferred_element_type=jnp.float32).astype(jnp.bfloat16),
        "dp",
        scatter_dimension=0,
        tiled=True,
    ).astype(jnp.float32)
    hidden = (jax.nn.silu(summed[:, :width]) * summed[:, width:]).astype(jnp.bfloat16)
    result = jnp.dot(
        lax.all_gather(hidden, "dp", axis=0, tiled=True),
        down_local,
        preferred_element_type=jnp.float32,
    )
    return result.astype(jnp.bfloat16)


def body(
    tokens, routes, gates, plan, proj_weight, proj_grad, first_moment, second_moment, down_weight
):
    owners = lax.axis_size("expert")
    updated = adam_update(proj_weight, proj_grad, first_moment, second_moment)[0]
    local_rows = updated.shape[1]
    width = updated.shape[2]
    group_tokens = tokens.shape[1]
    route_count = routes.shape[2]
    capacity = min(group_tokens, 3 * group_tokens * route_count // (2 * owners))
    down_local = down_weight[0]
    expert_ids = jnp.arange(owners, dtype=jnp.int32)
    route_list = routes[0]
    gate_list = gates[0]
    expert_match = route_list[:, :, None] == expert_ids[None, None, :]
    targets = jnp.sum(jnp.where(expert_match, plan[None, None, :], 0), axis=2)
    target_match = targets[:, :, None] == expert_ids[None, None, :]
    routed = jnp.sum(target_match.astype(jnp.int32), axis=1)
    weighting = jnp.sum(jnp.where(target_match, gate_list[:, :, None], 0.0), axis=1)
    ranks = jnp.cumsum(routed, axis=0) - routed
    slot_ids = jnp.arange(capacity, dtype=jnp.int32)
    select = jnp.logical_and(
        ranks.T[:, None, :] == slot_ids[None, :, None], routed.T[:, None, :] > 0
    )
    dispatch_buf = jnp.einsum(
        "ost,td->osd", select.astype(jnp.bfloat16), tokens[0], preferred_element_type=jnp.float32
    ).astype(jnp.bfloat16)
    proj_pieces = updated.reshape(2, owners, local_rows // owners, width)
    down_pieces = down_local.reshape(1, owners, width // owners, local_rows)
    arrived, spread_proj, spread_down = (
        lax.all_to_all(dispatch_buf[None], "expert", split_axis=1, concat_axis=1, tiled=True),
        lax.all_to_all(proj_pieces, "expert", split_axis=1, concat_axis=1, tiled=True),
        lax.all_to_all(down_pieces, "expert", split_axis=1, concat_axis=1, tiled=True),
    )
    moving = (plan[None, :] == expert_ids[:, None]).astype(jnp.bfloat16)
    placed_proj = jnp.einsum(
        "ox,axrf->aorf", moving, spread_proj, preferred_element_type=jnp.float32
    ).astype(jnp.bfloat16)
    placed_down = jnp.einsum(
        "ox,axrf->aorf", moving, spread_down, preferred_element_type=jnp.float32
    ).astype(jnp.bfloat16)
    slots = arrived.reshape(owners * capacity, local_rows)
    moved_proj, moved_down = (
        lax.all_to_all(placed_proj, "expert", split_axis=1, concat_axis=1, tiled=True),
        lax.all_to_all(placed_down, "expert", split_axis=1, concat_axis=1, tiled=True),
    )
    new_proj = moved_proj.reshape(2, local_rows, width)
    new_down = moved_down.reshape(width, local_rows)
    expert_out = expert_rows(slots, new_proj, new_down)
    returned = lax.all_to_all(
        expert_out.reshape(1, owners, capacity, local_rows),
        "expert",
        split_axis=1,
        concat_axis=1,
        tiled=True,
    )
    combine = select.astype(jnp.float32) * weighting.T[:, None, :]
    mixed = jnp.einsum(
        "ost,osd->td", combine, returned[0].astype(jnp.float32), precision=lax.Precision.HIGHEST
    )
    return (mixed.astype(jnp.bfloat16)[None], new_proj[None], new_down[None])


def solution(mesh):
    in_specs = (
        P("expert", None, "dp"),
        P("expert", None, None),
        P("expert", None, None),
        P(),
        P("expert", None, "dp", None),
        P("expert", None, "dp", None),
        P("expert", None, "dp", None),
        P("expert", None, "dp", None),
        P("expert", None, "dp"),
    )
    out_specs = (P("expert", None, "dp"), P("expert", None, "dp", None), P("expert", None, "dp"))
    return jax.shard_map(body, mesh=mesh, in_specs=in_specs, out_specs=out_specs, check_vma=False)
```

profile of v0, /device:TPU:0, one launch (start us, length us, event | category | flops | bytes accessed | tf_op | source)
XLA Modules:
  0.0 283.7 jit_solution(3105261243016543089)
XLA Ops:
  7.2 0.0 copy-start
  7.2 0.8 select_reduce_fusion.1
  8.0 0.1 copy.45
  8.1 0.1 copy.47
  8.2 0.0 copy-done
  8.2 1.0 fusion.26
  9.2 7.3 %all-to-all-start = ((bf16[1,8,16,1024]{3,2,0,1:T(8,128)(2,1)}), bf16[1,8,16,1024]{3,2,0,1:T(8,128)(2,1)S(1)}, u32[]{:S(2)}, u32[]{:S(2)}) async-start(bf16[1,8,16,1024]{3,2,0,1:T(8,128)(2,1)} %fusion.26), calls=%async_computation | async-start | bytes 524288 | tf_op jit(solution)/shard_map/all_to_all | solution.py:70
  16.5 9.0 %fusion.9 = bf16[1,2,1024,768]{3,2,1,0:T(8,128)(2,1)S(1)} fusion(f32[1,2,1024,768]{3,2,1,0:T(8,128)} %param.16, bf16[1,2,1024,768]{3,2,1,0:T(8,128)(2,1)} %param.14, f32[1,2,1024,768]{3,2,1,0:T(8,128)} %param.15, bf16[1,2,1024,768]{3,2,1,0:T(8,128)(2,1)} %param.13), kind=kLoop, calls=%fused_computation.11 | loop fusion | flops 25165824 | bytes 22020096 | tf_op jit(solution)/shard_map/convert_element_type | solution.py:19
  25.5 0.2 copy.50
  25.7 0.0 all-to-all-done
  25.7 76.2 %all_to_all.30 = bf16[2,8,128,768]{3,2,0,1:T(8,128)(2,1)} all-to-all(bf16[2,8,128,768]{3,2,0,1:T(8,128)(2,1)S(1)} %copy.50), channel_id=1, replica_groups=mesh['dp'=4,'expert'=8] {'expert'}, dimensions={1} | all-to-all | bytes 6291456 | tf_op jit(solution)/shard_map/all_to_all | solution.py:71
  101.9 0.0 copy-start.1
  101.9 0.0 copy-start.2
  101.9 4.6 %all-to-all-start.3 = ((bf16[1,8,96,1024]{3,2,0,1:T(8,128)(2,1)}), bf16[1,8,96,1024]{3,2,0,1:T(8,128)(2,1)}, u32[]{:S(2)}, u32[]{:S(2)}) async-start(bf16[1,8,96,1024]{3,2,0,1:T(8,128)(2,1)} %bitcast.65), calls=%async_computation.4 | async-start | bytes 3145728 | tf_op jit(solution)/shard_map/all_to_all | solution.py:72
  106.5 0.0 copy-done.1
  106.5 0.0 copy-done.2
  106.5 2.0 convert_bitcast_fusion
  108.5 2.3 copy.52
  110.9 31.7 %all-to-all-done.3 = bf16[1,8,96,1024]{3,2,0,1:T(8,128)(2,1)} async-done(((bf16[1,8,96,1024]{3,2,0,1:T(8,128)(2,1)}), bf16[1,8,96,1024]{3,2,0,1:T(8,128)(2,1)}, u32[]{:S(2)}, u32[]{:S(2)}) %all-to-all-start.3) | async-done | bytes 1572896 | tf_op jit(solution)/shard_map/all_to_all | solution.py:72
  142.6 3.7 %all-to-all-start.2 = ((bf16[2,8,128,768]{3,2,0,1:T(8,128)(2,1)}), bf16[2,8,128,768]{3,2,0,1:T(8,128)(2,1)S(1)}, u32[]{:S(2)}, u32[]{:S(2)}) async-start(bf16[2,8,128,768]{3,2,0,1:T(8,128)(2,1)} %copy.52), calls=%async_computation.2 | async-start | bytes 6291456 | tf_op jit(solution)/shard_map/all_to_all | solution.py:83
  146.2 2.4 fusion.23
  148.7 2.0 copy.57
  150.7 66.2 %all-to-all-done.2 = bf16[2,8,128,768]{3,2,0,1:T(8,128)(2,1)S(1)} async-done(((bf16[2,8,128,768]{3,2,0,1:T(8,128)(2,1)}), bf16[2,8,128,768]{3,2,0,1:T(8,128)(2,1)S(1)}, u32[]{:S(2)}, u32[]{:S(2)}) %all-to-all-start.2) | async-done | bytes 3145760 | tf_op jit(solution)/shard_map/all_to_all | solution.py:83
  216.9 4.3 %all-to-all-start.4 = ((bf16[1,8,96,1024]{3,2,0,1:T(8,128)(2,1)}), bf16[1,8,96,1024]{3,2,0,1:T(8,128)(2,1)}, u32[]{:S(2)}, u32[]{:S(2)}) async-start(bf16[1,8,96,1024]{3,2,0,1:T(8,128)(2,1)} %copy.57), calls=%async_computation.5 | async-start | bytes 3145728 | tf_op jit(solution)/shard_map/all_to_all | solution.py:84
  221.2 0.0 reduce-scatter.2.cloned.1.call-start
  221.2 0.2 fusion.50
  221.5 1.3 fusion.16
  222.8 0.0 copy-start.3
  222.8 0.0 reduce-scatter.2.cloned.1.call-update
  222.9 24.4 %reduce-scatter.2.cloned.1.call-done = bf16[32,1536]{1,0:T(8,128)(2,1)} async-done(((bf16[128,1536]{1,0:T(8,128)(2,1)}), bf16[32,1536]{1,0:T(8,128)(2,1)}) %reduce-scatter.2.cloned.1.call-update) | async-done | bytes 98320 | tf_op jit(solution)/shard_map/reduce_scatter | solution.py:25
  247.3 0.9 convert_element_type.60
  248.2 5.6 %all_gather.3 = bf16[128,768]{1,0:T(8,128)(2,1)S(1)} all-gather(bf16[32,768]{1,0:T(8,128)(2,1)S(1)} %fusion.30), channel_id=1, replica_groups=mesh['dp'=4,'expert'=8] {'dp'}, dimensions={0}, use_global_device_ids=true | all-gather | bytes 245760 | tf_op jit(solution)/shard_map/all_gather | solution.py:33
  253.8 4.0 %all-to-all-done.4 = bf16[1,8,96,1024]{3,2,0,1:T(8,128)(2,1)} async-done(((bf16[1,8,96,1024]{3,2,0,1:T(8,128)(2,1)}), bf16[1,8,96,1024]{3,2,0,1:T(8,128)(2,1)}, u32[]{:S(2)}, u32[]{:S(2)}) %all-to-all-start.4) | async-done | bytes 1572896 | tf_op jit(solution)/shard_map/all_to_all | solution.py:84
  257.8 2.5 convolution_convert_fusion.2
  260.3 3.6 %all-to-all-start.5 = ((bf16[1,8,16,1024]{3,2,0,1:T(8,128)(2,1)}), bf16[1,8,16,1024]{3,2,0,1:T(8,128)(2,1)S(1)}, u32[]{:S(2)}, u32[]{:S(2)}) async-start(bf16[1,8,16,1024]{3,2,0,1:T(8,128)(2,1)} %bitcast.25), calls=%async_computation.6 | async-start | bytes 524288 | tf_op jit(solution)/shard_map/all_to_all | solution.py:89
  264.0 0.0 copy-done.3
  264.0 1.9 copy.53
  265.9 7.2 %all-to-all-done.5 = bf16[1,8,16,1024]{3,2,0,1:T(8,128)(2,1)S(1)} async-done(((bf16[1,8,16,1024]{3,2,0,1:T(8,128)(2,1)}), bf16[1,8,16,1024]{3,2,0,1:T(8,128)(2,1)S(1)}, u32[]{:S(2)}, u32[]{:S(2)}) %all-to-all-start.5) | async-done | bytes 262176 | tf_op jit(solution)/shard_map/all_to_all | solution.py:89
  273.1 1.1 fusion.28
  274.2 2.7 copy.75
  (6 shorter events, 0.1 us)
Async XLA Ops:
  7.2 1.0 copy-start
  9.2 16.5 %all-to-all-start = ((bf16[1,8,16,1024]{3,2,0,1:T(8,128)(2,1)}), bf16[1,8,16,1024]{3,2,0,1:T(8,128)(2,1)S(1)}, u32[]{:S(2)}, u32[]{:S(2)}) async-start(bf16[1,8,16,1024]{3,2,0,1:T(8,128)(2,1)} %fusion.26), calls=%async_computation | async-start | bytes 524288 | tf_op jit(solution)/shard_map/all_to_all | solution.py:70
  101.9 4.6 %copy-start.1 = (bf16[2,8,128,768]{3,2,0,1:T(8,128)(2,1)S(1)}, bf16[2,8,128,768]{3,2,0,1:T(8,128)(2,1)}, u32[]{:S(2)}) copy-start(bf16[2,8,128,768]{3,2,0,1:T(8,128)(2,1)} %all_to_all.30) | copy-start | bytes 9437188
  101.9 4.6 %copy-start.2 = (s32[8]{0:T(128)S(1)}, s32[8]{0:T(128)}, u32[]{:S(2)}) copy-start(s32[8]{0:T(128)} %param.12) | copy-start | bytes 100
  101.9 40.7 %all-to-all-start.3 = ((bf16[1,8,96,1024]{3,2,0,1:T(8,128)(2,1)}), bf16[1,8,96,1024]{3,2,0,1:T(8,128)(2,1)}, u32[]{:S(2)}, u32[]{:S(2)}) async-start(bf16[1,8,96,1024]{3,2,0,1:T(8,128)(2,1)} %bitcast.65), calls=%async_computation.4 | async-start | bytes 3145728 | tf_op jit(solution)/shard_map/all_to_all | solution.py:72
  142.6 74.3 %all-to-all-start.2 = ((bf16[2,8,128,768]{3,2,0,1:T(8,128)(2,1)}), bf16[2,8,128,768]{3,2,0,1:T(8,128)(2,1)S(1)}, u32[]{:S(2)}, u32[]{:S(2)}) async-start(bf16[2,8,128,768]{3,2,0,1:T(8,128)(2,1)} %copy.52), calls=%async_computation.2 | async-start | bytes 6291456 | tf_op jit(solution)/shard_map/all_to_all | solution.py:83
  216.9 40.9 %all-to-all-start.4 = ((bf16[1,8,96,1024]{3,2,0,1:T(8,128)(2,1)}), bf16[1,8,96,1024]{3,2,0,1:T(8,128)(2,1)}, u32[]{:S(2)}, u32[]{:S(2)}) async-start(bf16[1,8,96,1024]{3,2,0,1:T(8,128)(2,1)} %copy.57), calls=%async_computation.5 | async-start | bytes 3145728 | tf_op jit(solution)/shard_map/all_to_all | solution.py:84
  221.2 26.1 %reduce-scatter.2.cloned.1.call-start = ((), (), s32[]{:S(2)}) async-start(), calls=%async_computation.7 | async-start | bytes 491520 | tf_op jit(solution)/shard_map/reduce_scatter | solution.py:25
  222.8 41.1 %copy-start.3 = (f32[1,16,8]{1,2,0:T(8,128)S(1)}, f32[1,16,8]{1,2,0:T(8,128)}, u32[]{:S(2)}) copy-start(f32[1,16,8]{1,2,0:T(8,128)} %param.11) | copy-start | bytes 1540
  260.3 12.7 %all-to-all-start.5 = ((bf16[1,8,16,1024]{3,2,0,1:T(8,128)(2,1)}), bf16[1,8,16,1024]{3,2,0,1:T(8,128)(2,1)S(1)}, u32[]{:S(2)}, u32[]{:S(2)}) async-start(bf16[1,8,16,1024]{3,2,0,1:T(8,128)(2,1)} %bitcast.25), calls=%async_computation.6 | async-start | bytes 524288 | tf_op jit(solution)/shard_map/all_to_all | solution.py:89
Sparse Core Ops, SparseCore 0:
  225.1 22.1 reduce-scatter.1
where the time goes:
time: 284 us
  waiting for transfers between devices  134 us (47%)
  blocking collectives  81.8 us (29%)
  starting transfers between devices  23.4 us (8%)
  between operations  14.2 us (5%)
  other arithmetic  10.8 us (4%)
  matrix products  10.5 us (4%)
  local copies, waits for them, and re-layouts  9.52 us (3%)
    all_to_all x1, blocking collectives, body(): lax.all_to_all(proj_pieces, 'expert', split_axis=1, concat_axis=1, tiled=...  76.2 us
    all_to_all x1, waiting for transfers between devices, body(): lax.all_to_all(placed_proj, 'expert', split_axis=1, concat_axis=1, tiled=...  66.2 us
    all_to_all x1, waiting for transfers between devices, body(): lax.all_to_all(down_pieces, 'expert', split_axis=1, concat_axis=1, tiled=...  31.7 us
    reduce_scatter x1, waiting for transfers between devices, expert_rows(): lax.psum_scatter(jnp.dot(slots, joined, preferred_element_type=jnp.float3...  24.4 us
    convert_element_type x1, other arithmetic, adam_update(): (weights.astype(jnp.float32) - learning_rate * adam_step).astype(jnp.bflo...  9.01 us
    all_to_all x1, starting transfers between devices, body(): lax.all_to_all(dispatch_buf[None], 'expert', split_axis=1, concat_axis=1,...  7.25 us
    all_to_all x1, waiting for transfers between devices, body(): lax.all_to_all(expert_out.reshape(1, owners, capacity, local_rows), 'expe...  7.19 us
  transfers between devices with their start and end apart: 6, of which 5 were waited for; matrix products, arithmetic and copies ran while one was open for 8% of the time, Pallas kernels for 0%

commit v1 on v0

v1 whole, which is shorter than its diff:
```python
import itertools

import jax
import jax.numpy as jnp
import numpy as np
from jax import lax
from jax.sharding import PartitionSpec as P

learning_rate = 0.01
beta_first = 0.9
beta_second = 0.999
adam_epsilon = 1e-08
bias_first = 1.0 - 0.9**10
bias_second = 1.0 - 0.999**10


def adam_update(weights, grads, first_moment, second_moment):
    grad_float = grads.astype(jnp.float32)
    first_new = beta_first * first_moment + (1.0 - beta_first) * grad_float
    second_new = beta_second * second_moment + (1.0 - beta_second) * grad_float * grad_float
    adam_step = first_new / bias_first / (jnp.sqrt(second_new / bias_second) + adam_epsilon)
    return (weights.astype(jnp.float32) - learning_rate * adam_step).astype(jnp.bfloat16)


max_levels = 1


def partial_products(slots, updated):
    joined = jnp.concatenate([updated[0], updated[1]], axis=1)
    return jnp.dot(slots, joined, preferred_element_type=jnp.float32).astype(jnp.bfloat16)


def finish_rows(partials, down_local):
    width = down_local.shape[0]
    parts = lax.axis_size("dp")
    blocks = lax.all_to_all(
        partials.reshape(1, parts, -1, partials.shape[1]),
        "dp",
        split_axis=1,
        concat_axis=1,
        tiled=True,
    )
    summed = jnp.sum(blocks[0].astype(jnp.float32), axis=0)
    hidden = (jax.nn.silu(summed[:, :width]) * summed[:, width:]).astype(jnp.bfloat16)
    result = jnp.dot(
        lax.all_gather(hidden, "dp", axis=0, tiled=True),
        down_local,
        preferred_element_type=jnp.float32,
    )
    return result.astype(jnp.bfloat16)


def owner_exchange(pieces):
    return lax.all_to_all(pieces, "expert", split_axis=1, concat_axis=1, tiled=True)


def two_phase_migration(plan, updated, down_local):
    owners = lax.axis_size("expert")
    local_rows, width = updated.shape[1:]
    expert_ids = jnp.arange(owners, dtype=jnp.int32)
    spread_down = owner_exchange(down_local.reshape(1, owners, width // owners, local_rows))
    spread_proj = owner_exchange(updated.reshape(2, owners, local_rows // owners, width))
    inverse = jnp.sum(
        jnp.where(plan[None, :] == expert_ids[:, None], expert_ids[None, :], 0), axis=1
    )
    moved_down = owner_exchange(jnp.take(spread_down, inverse, axis=1))
    moved_proj = owner_exchange(jnp.take(spread_proj, inverse, axis=1))
    return moved_proj.reshape(2, local_rows, width), moved_down.reshape(width, local_rows)


def colour_table(levels):
    bits = np.array(list(itertools.product((0, 1), repeat=levels)), np.int32)
    return np.stack([bits, 1 - bits], axis=2).reshape(len(bits), 2 * levels)


def worst_cut(perm):
    worst = 0
    for cut in range(1, len(perm)):
        up = sum(1 for z, to in enumerate(perm) if z < cut <= to)
        worst = max(worst, up)
    return worst


def route_choice(plan, levels):
    owners = 2 * levels
    perms = list(itertools.permutations(range(levels)))
    colours = colour_table(levels)
    ids = jnp.arange(owners, dtype=jnp.int32)
    arrives = plan[:, None] == ids[None, :]
    landed = jnp.sum(jnp.where(arrives[None], colours[:, :, None], 0), axis=1)
    pair_sum = landed.reshape(-1, levels, 2).sum(axis=2)
    bad = jnp.sum((pair_sum != 1).astype(jnp.int32), axis=1)
    scale = np.repeat(levels ** np.arange(levels, dtype=np.int32), 2)
    term = (plan // 2) * scale
    codes = np.array([sum(to * levels**z for z, to in enumerate(p)) for p in perms], np.int32)
    costs = np.array([worst_cut(p) for p in perms], np.int32)
    keys = [
        jnp.sum(jnp.where(colours == colour, term[None, :], 0), axis=1) for colour in (0, 1)
    ]
    hits = [key[:, None] == codes[None, :] for key in keys]
    cost = sum(jnp.sum(jnp.where(hit, costs[None, :], 0), axis=1) for hit in hits)
    count = len(colours)
    order = (bad * (4 * levels) + cost) * count + jnp.arange(count, dtype=jnp.int32)
    chosen = jnp.arange(count, dtype=jnp.int32) == jnp.min(order) % count
    numbers = np.arange(len(perms), dtype=np.int32)
    picks = [
        jnp.sum(jnp.where(chosen[:, None] & hit, numbers[None, :], 0)) for hit in hits
    ]
    source = jnp.sum(jnp.where(chosen[:, None], colours, 0), axis=0)
    landing = jnp.sum(jnp.where(chosen[:, None], landed, 0), axis=0)
    return source, landing, picks, perms


def body(
    tokens, routes, gates, plan, proj_weight, proj_grad, first_moment, second_moment, down_weight
):
    owners = lax.axis_size("expert")
    updated = adam_update(proj_weight, proj_grad, first_moment, second_moment)[0]
    local_rows = updated.shape[1]
    width = updated.shape[2]
    group_tokens = tokens.shape[1]
    route_count = routes.shape[2]
    capacity = min(group_tokens, 3 * group_tokens * route_count // (2 * owners))
    down_local = down_weight[0]
    expert_ids = jnp.arange(owners, dtype=jnp.int32)
    target_match = routes[0][:, :, None] == expert_ids[None, None, :]
    routed = jnp.sum(target_match.astype(jnp.int32), axis=1)
    weighting = jnp.sum(jnp.where(target_match, gates[0][:, :, None], 0.0), axis=1)
    ranks = jnp.cumsum(routed, axis=0) - routed
    slot_ids = jnp.arange(capacity, dtype=jnp.int32)
    select = jnp.logical_and(
        ranks.T[:, None, :] == slot_ids[None, :, None], routed.T[:, None, :] > 0
    )
    dispatch_buf = jnp.einsum(
        "ost,td->osd", select.astype(jnp.bfloat16), tokens[0], preferred_element_type=jnp.float32
    ).astype(jnp.bfloat16)
    arrived = owner_exchange(dispatch_buf[None])
    slots = arrived.reshape(owners * capacity, local_rows)

    def experts(partials):
        expert_out = finish_rows(partials, down_local)
        return owner_exchange(expert_out.reshape(1, owners, capacity, local_rows))

    levels = owners // 2
    if levels > max_levels:
        new_proj, new_down = two_phase_migration(plan, updated, down_local)
        returned = experts(partial_products(slots, updated))
    else:
        new_proj, new_down, returned = routed_migration(
            plan, levels, updated, down_local, slots, experts
        )
    combine = select.astype(jnp.float32) * weighting.T[:, None, :]
    mixed = jnp.einsum(
        "ost,osd->td", combine, returned[0].astype(jnp.float32), precision=lax.Precision.HIGHEST
    )
    return (mixed.astype(jnp.bfloat16)[None], new_proj[None], new_down[None])


def routed_migration(plan, levels, updated, down_local, slots, experts):
    source, landing, picks, perms = route_choice(plan, levels)
    me = lax.axis_index("expert")
    line = me % 2
    at_me = jnp.arange(2 * levels, dtype=jnp.int32) == me
    colour = jnp.sum(jnp.where(at_me, source, 0))
    landing_colour = jnp.sum(jnp.where(at_me, landing, 0))
    kept_half = line ^ colour
    final_half = line ^ landing_colour
    across = [(e, e ^ 1) for e in range(2 * levels)]
    local_rows, width = updated.shape[1:]
    piece = local_rows // 2

    def swap(value):
        return lax.ppermute(value, "expert", across)

    def parted(halves):
        keep = jnp.where(kept_half == 0, halves[0], halves[1])
        send = jnp.where(kept_half == 0, halves[1], halves[0])
        return keep, send

    def coloured(keep, other):
        first = jnp.where(colour == 0, keep, other)
        second = jnp.where(colour == 0, other, keep)
        return first, second

    down_halves = down_local.reshape(2, width // 2, local_rows)
    keep, send = parted(down_halves)
    down_first, down_second = coloured(keep, swap(send))
    proj_parts = [
        parted(updated[:, i * piece : (i + 1) * piece]) for i in range(2)
    ]
    partials = partial_products(slots, updated)

    def along(perm):
        pairs = [(2 * z + x, 2 * to + x) for z, to in enumerate(perm) for x in (0, 1)]
        return lambda value: lax.ppermute(value, "expert", pairs)

    def first_stage(perm):
        move = along(perm)

        def run(down_first, proj_parts, partials):
            moved_down = move(down_first)
            moved, waiting = [], []
            for keep, send in proj_parts:
                first, second = coloured(keep, swap(send))
                moved.append(move(first))
                waiting.append(second)
            return moved_down, moved, waiting, experts(partials)

        return run

    def second_stage(perm):
        move = along(perm)

        def run(items, moved):
            landed = []
            for first, waiting in zip(moved, items):
                second = move(waiting)
                keep = jnp.where(landing_colour == 0, first, second)
                send = jnp.where(landing_colour == 0, second, first)
                other = swap(send)
                landed.append(
                    (
                        jnp.where(final_half == 0, keep, other),
                        jnp.where(final_half == 0, other, keep),
                    )
                )
            return landed

        return run

    moved_down, moved, waiting, returned = lax.switch(
        picks[0], [first_stage(p) for p in perms], down_first, proj_parts, partials
    )
    landed = lax.switch(
        picks[1],
        [second_stage(p) for p in perms],
        [down_second] + waiting,
        [moved_down] + moved,
    )
    new_down = jnp.concatenate(landed[0], axis=0)
    new_proj = jnp.stack(
        [jnp.concatenate([pair[h] for pair in landed[1:]], axis=0) for h in (0, 1)]
    )
    return new_proj, new_down, returned


def solution(mesh):
    in_specs = (
        P("expert", None, "dp"),
        P("expert", None, None),
        P("expert", None, None),
        P(),
        P("expert", None, "dp", None),
        P("expert", None, "dp", None),
        P("expert", None, "dp", None),
        P("expert", None, "dp", None),
        P("expert", None, "dp"),
    )
    out_specs = (P("expert", None, "dp"), P("expert", None, "dp", None), P("expert", None, "dp"))
    return jax.shard_map(body, mesh=mesh, in_specs=in_specs, out_specs=out_specs, check_vma=False)
```

time: 284 us -> 291 us (1.025)
  waiting for transfers between devices: 134 us -> 199 us
  blocking collectives: 81.8 us -> 30.9 us
  between operations: 14.2 us -> 0.76 us
  local copies, waits for them, and re-layouts: 9.52 us -> 16.2 us
  matrix products: 10.5 us -> 5.15 us
  other arithmetic: 10.8 us -> 14.8 us
    all_to_all x5, waiting for transfers between devices: 109 us -> 199 us  [owner_exchange(): lax.all_to_all(pieces, 'expert', split_axis=1, concat_axis=1, tiled=True)]
    all_to_all x1 -> x2, blocking collectives: 76.2 us -> 25.2 us  [the longest x1 15.2 us: owner_exchange(): lax.all_to_all(pieces, 'expert', split_axis=1, concat_axis=1, tiled=True)]
    reduce_scatter x1 -> x0, waiting for transfers between devices: 24.4 us -> none  [expert_rows(): lax.psum_scatter(jnp.dot(slots, joined, preferred_element_type=jnp.float3...]
    gather x0 -> x2, local copies, waits for them, and re-layouts: none -> 5.83 us  [the longest x1 3.2 us: two_phase_migration(): moved_down = owner_exchange(jnp.take(spread_down, inverse, axis=1))]
    dot_general x4 -> x2, matrix products: 8.26 us -> 2.98 us  [the longest x1 2.58 us: partial_products(): jnp.dot(slots, joined, preferred_element_type=jnp.float32)]
    select_n x0 -> x3, other arithmetic: none -> 4.8 us  [the longest x1 2.76 us: two_phase_migration(): moved_down = owner_exchange(jnp.take(spread_down, inverse, axis=1))]
    convert_element_type x2 -> x0, local copies, waits for them, and re-layouts: 4.34 us -> none  [the longest x1 2.32 us: body(): placed_proj = jnp.einsum('ox,axrf->aorf', moving, spread_proj, preferred_...]
  transfers between devices with their start and end apart: 6 -> 5, of which waited for: 5 -> 4; matrix products, arithmetic and copies ran while one was open for 8% -> 9% of each run, Pallas kernels for 0% -> 0%
where the time goes in v1:
time: 291 us; the launch traced here: 290 us
  waiting for transfers between devices  199 us (68%)
  blocking collectives  30.9 us (11%)
  starting transfers between devices  23.1 us (8%)
  local copies, waits for them, and re-layouts  16.2 us (6%)
  other arithmetic  14.8 us (5%)
  matrix products  5.15 us (2%)
    all_to_all x5, waiting for transfers between devices, owner_exchange(): lax.all_to_all(pieces, 'expert', split_axis=1, concat_axis=1, tiled=True)  199 us
    all_to_all x5, starting transfers between devices, owner_exchange(): lax.all_to_all(pieces, 'expert', split_axis=1, concat_axis=1, tiled=True)  23.1 us
    all_to_all x1, blocking collectives, owner_exchange(): lax.all_to_all(pieces, 'expert', split_axis=1, concat_axis=1, tiled=True)  15.2 us
    all_to_all x1, blocking collectives, finish_rows(): lax.all_to_all(partials.reshape(1, parts, -1, partials.shape[1]), 'dp', s...  10 us
    convert_element_type x1, other arithmetic, adam_update(): (weights.astype(jnp.float32) - learning_rate * adam_step).astype(jnp.bflo...  9.01 us
  transfers between devices with their start and end apart: 5, of which 4 were waited for; matrix products, arithmetic and copies ran while one was open for 9% of the time, Pallas kernels for 0%

profile of v1, /device:TPU:0, one launch (start us, length us, event | category | flops | bytes accessed | tf_op | source)
XLA Modules:
  0.0 290.0 jit_solution(9673532257197354397)
XLA Ops:
  0.6 0.0 copy-start
  0.6 0.7 convert_reduce_fusion.1
  1.4 0.1 copy.51
  1.5 0.1 copy.53
  1.5 0.0 copy-done
  1.5 1.0 fusion.23
  2.6 7.3 %all-to-all-start = ((bf16[1,8,16,1024]{3,2,0,1:T(8,128)(2,1)}), bf16[1,8,16,1024]{3,2,0,1:T(8,128)(2,1)S(1)}, u32[]{:S(2)}, u32[]{:S(2)}) async-start(bf16[1,8,16,1024]{3,2,0,1:T(8,128)(2,1)} %fusion.23), calls=%async_computation | async-start | bytes 524288 | tf_op jit(solution)/shard_map/all_to_all | solution.py:54
  9.8 9.0 %fusion.9 = bf16[1,2,1024,768]{3,2,1,0:T(8,128)(2,1)S(1)} fusion(f32[1,2,1024,768]{3,2,1,0:T(8,128)} %param.16, bf16[1,2,1024,768]{3,2,1,0:T(8,128)(2,1)} %param.14, f32[1,2,1024,768]{3,2,1,0:T(8,128)} %param.15, bf16[1,2,1024,768]{3,2,1,0:T(8,128)(2,1)} %param.13), kind=kLoop, calls=%fused_computation.13 | loop fusion | flops 25165824 | bytes 22020096 | tf_op jit(solution)/shard_map/convert_element_type | solution.py:22
  18.8 1.9 slice_bitcast_fusion.1
  20.7 0.0 all-to-all-done
  20.7 0.0 copy-start.1
  20.7 2.6 fusion.14
  23.3 10.0 %all_to_all.35 = bf16[1,4,32,1536]{3,2,0,1:T(8,128)(2,1)S(1)} all-to-all(bf16[1,4,32,1536]{3,2,0,1:T(8,128)(2,1)S(1)} %bitcast.65), channel_id=1, replica_groups=mesh['dp'=4,'expert'=8] {'dp'}, dimensions={1} | all-to-all | bytes 786432 | tf_op jit(solution)/shard_map/all_to_all | solution.py:36
  33.3 0.1 convert_reduce_fusion
  33.4 5.6 %all_gather.3 = bf16[128,768]{1,0:T(8,128)(2,1)S(1)} all-gather(bf16[32,768]{1,0:T(8,128)(2,1)S(1)} %fusion.27), channel_id=1, replica_groups=mesh['dp'=4,'expert'=8] {'dp'}, dimensions={0}, use_global_device_ids=true | all-gather | bytes 245760 | tf_op jit(solution)/shard_map/all_gather | solution.py:46
  39.0 0.0 copy-done.1
  39.0 0.4 fusion.20
  39.4 15.2 %all_to_all.36 = bf16[1,8,16,1024]{3,2,0,1:T(8,128)(2,1)S(1)} all-to-all(bf16[1,8,16,1024]{3,2,0,1:T(8,128)(2,1)S(1)} %bitcast.64), channel_id=1, replica_groups=mesh['dp'=4,'expert'=8] {'expert'}, dimensions={1} | all-to-all | bytes 524288 | tf_op jit(solution)/shard_map/all_to_all | solution.py:54
  54.7 4.3 %all-to-all-start.5 = ((bf16[1,8,96,1024]{3,2,0,1:T(8,128)(2,1)}), bf16[1,8,96,1024]{3,2,0,1:T(8,128)(2,1)}, u32[]{:S(2)}, u32[]{:S(2)}) async-start(bf16[1,8,96,1024]{3,2,0,1:T(8,128)(2,1)} %bitcast.62), calls=%async_computation.5 | async-start | bytes 3145728 | tf_op jit(solution)/shard_map/all_to_all | solution.py:54
  59.0 1.9 copy.58
  60.8 0.0 copy-start.4
  60.8 34.6 %all-to-all-done.5 = bf16[1,8,96,1024]{3,2,0,1:T(8,128)(2,1)} async-done(((bf16[1,8,96,1024]{3,2,0,1:T(8,128)(2,1)}), bf16[1,8,96,1024]{3,2,0,1:T(8,128)(2,1)}, u32[]{:S(2)}, u32[]{:S(2)}) %all-to-all-start.5) | async-done | bytes 1572896 | tf_op jit(solution)/shard_map/all_to_all | solution.py:54
  95.4 3.7 %all-to-all-start.3 = ((bf16[2,8,128,768]{3,2,0,1:T(8,128)(2,1)}), bf16[2,8,128,768]{3,2,0,1:T(8,128)(2,1)S(1)}, u32[]{:S(2)}, u32[]{:S(2)}) async-start(bf16[2,8,128,768]{3,2,0,1:T(8,128)(2,1)} %copy.58), calls=%async_computation.3 | async-start | bytes 6291456 | tf_op jit(solution)/shard_map/all_to_all | solution.py:54
  99.1 0.0 copy-done.4
  99.1 0.1 select_reduce_fusion.1
  99.3 3.2 %gather_fusion.1 = bf16[8,96,1024]{2,1,0:T(8,128)(2,1)} fusion(bf16[8,96,1024]{2,1,0:T(8,128)(2,1)} %bitcast.26, s32[1024]{0:T(1024)S(1)} %pad_clamp_fusion), kind=kCustom, calls=%fused_computation.1 | custom fusion | bytes 3145760 | tf_op jit(solution)/shard_map/jit(_take)/gather | solution.py:66
  102.5 2.8 fusion.17
  105.2 64.7 %all-to-all-done.3 = bf16[2,8,128,768]{3,2,0,1:T(8,128)(2,1)S(1)} async-done(((bf16[2,8,128,768]{3,2,0,1:T(8,128)(2,1)}), bf16[2,8,128,768]{3,2,0,1:T(8,128)(2,1)S(1)}, u32[]{:S(2)}, u32[]{:S(2)}) %all-to-all-start.3) | async-done | bytes 3145760 | tf_op jit(solution)/shard_map/all_to_all | solution.py:54
  170.0 4.3 %all-to-all-start.6 = ((bf16[1,8,96,1024]{3,2,0,1:T(8,128)(2,1)}), bf16[1,8,96,1024]{3,2,0,1:T(8,128)(2,1)}, u32[]{:S(2)}, u32[]{:S(2)}) async-start(bf16[1,8,96,1024]{3,2,0,1:T(8,128)(2,1)} %fusion.17), calls=%async_computation.6 | async-start | bytes 3145728 | tf_op jit(solution)/shard_map/all_to_all | solution.py:54
  174.2 1.9 copy.59
  176.1 2.6 gather_fusion
  178.8 2.0 select_bitcast_fusion
  180.8 0.0 copy-start.2
  180.8 0.0 copy-start.3
  180.8 30.1 %all-to-all-done.6 = bf16[1,8,96,1024]{3,2,0,1:T(8,128)(2,1)} async-done(((bf16[1,8,96,1024]{3,2,0,1:T(8,128)(2,1)}), bf16[1,8,96,1024]{3,2,0,1:T(8,128)(2,1)}, u32[]{:S(2)}, u32[]{:S(2)}) %all-to-all-start.6) | async-done | bytes 1572896 | tf_op jit(solution)/shard_map/all_to_all | solution.py:54
  210.9 3.7 %all-to-all-start.4 = ((bf16[2,8,128,768]{3,2,0,1:T(8,128)(2,1)}), bf16[2,8,128,768]{3,2,0,1:T(8,128)(2,1)S(1)}, u32[]{:S(2)}, u32[]{:S(2)}) async-start(bf16[2,8,128,768]{3,2,0,1:T(8,128)(2,1)} %select_bitcast_fusion), calls=%async_computation.4 | async-start | bytes 6291456 | tf_op jit(solution)/shard_map/all_to_all | solution.py:54
  214.6 0.0 copy-done.2
  214.6 0.0 copy-done.3
  214.6 1.1 fusion.25
  215.8 69.7 %all-to-all-done.4 = bf16[2,8,128,768]{3,2,0,1:T(8,128)(2,1)S(1)} async-done(((bf16[2,8,128,768]{3,2,0,1:T(8,128)(2,1)}), bf16[2,8,128,768]{3,2,0,1:T(8,128)(2,1)S(1)}, u32[]{:S(2)}, u32[]{:S(2)}) %all-to-all-start.4) | async-done | bytes 3145760 | tf_op jit(solution)/shard_map/all_to_all | solution.py:54
  285.4 1.9 copy.60
  287.3 2.7 copy.64
  (8 shorter events, 0.1 us)
Async XLA Ops:
  0.6 0.9 copy-start
  2.6 18.1 %all-to-all-start = ((bf16[1,8,16,1024]{3,2,0,1:T(8,128)(2,1)}), bf16[1,8,16,1024]{3,2,0,1:T(8,128)(2,1)S(1)}, u32[]{:S(2)}, u32[]{:S(2)}) async-start(bf16[1,8,16,1024]{3,2,0,1:T(8,128)(2,1)} %fusion.23), calls=%async_computation | async-start | bytes 524288 | tf_op jit(solution)/shard_map/all_to_all | solution.py:54
  20.7 18.3 %copy-start.1 = (bf16[1,768,1024]{2,1,0:T(8,128)(2,1)S(1)}, bf16[1,768,1024]{2,1,0:T(8,128)(2,1)}, u32[]{:S(2)}) copy-start(bf16[1,768,1024]{2,1,0:T(8,128)(2,1)} %param.17) | copy-start | bytes 4718596
  54.7 40.8 %all-to-all-start.5 = ((bf16[1,8,96,1024]{3,2,0,1:T(8,128)(2,1)}), bf16[1,8,96,1024]{3,2,0,1:T(8,128)(2,1)}, u32[]{:S(2)}, u32[]{:S(2)}) async-start(bf16[1,8,96,1024]{3,2,0,1:T(8,128)(2,1)} %bitcast.62), calls=%async_computation.5 | async-start | bytes 3145728 | tf_op jit(solution)/shard_map/all_to_all | solution.py:54
  60.8 38.3 %copy-start.4 = (s32[8]{0:T(128)S(1)}, s32[8]{0:T(128)}, u32[]{:S(2)}) copy-start(s32[8]{0:T(128)} %param.12) | copy-start | bytes 100
  95.4 74.5 %all-to-all-start.3 = ((bf16[2,8,128,768]{3,2,0,1:T(8,128)(2,1)}), bf16[2,8,128,768]{3,2,0,1:T(8,128)(2,1)S(1)}, u32[]{:S(2)}, u32[]{:S(2)}) async-start(bf16[2,8,128,768]{3,2,0,1:T(8,128)(2,1)} %copy.58), calls=%async_computation.3 | async-start | bytes 6291456 | tf_op jit(solution)/shard_map/all_to_all | solution.py:54
  170.0 40.9 %all-to-all-start.6 = ((bf16[1,8,96,1024]{3,2,0,1:T(8,128)(2,1)}), bf16[1,8,96,1024]{3,2,0,1:T(8,128)(2,1)}, u32[]{:S(2)}, u32[]{:S(2)}) async-start(bf16[1,8,96,1024]{3,2,0,1:T(8,128)(2,1)} %fusion.17), calls=%async_computation.6 | async-start | bytes 3145728 | tf_op jit(solution)/shard_map/all_to_all | solution.py:54
  180.8 33.8 %copy-start.2 = (s32[1,16,8]{1,2,0:T(8,128)S(1)}, s32[1,16,8]{1,2,0:T(8,128)}, u32[]{:S(2)}) copy-start(s32[1,16,8]{1,2,0:T(8,128)} %param.10) | copy-start | bytes 1540
  180.8 33.8 %copy-start.3 = (f32[1,16,8]{1,2,0:T(8,128)S(1)}, f32[1,16,8]{1,2,0:T(8,128)}, u32[]{:S(2)}) copy-start(f32[1,16,8]{1,2,0:T(8,128)} %param.11) | copy-start | bytes 1540
  210.9 74.5 %all-to-all-start.4 = ((bf16[2,8,128,768]{3,2,0,1:T(8,128)(2,1)}), bf16[2,8,128,768]{3,2,0,1:T(8,128)(2,1)S(1)}, u32[]{:S(2)}, u32[]{:S(2)}) async-start(bf16[2,8,128,768]{3,2,0,1:T(8,128)(2,1)} %select_bitcast_fusion), calls=%async_computation.4 | async-start | bytes 6291456 | tf_op jit(solution)/shard_map/all_to_all | solution.py:54

commit v2 on v1

--- a/solution.py
+++ b/solution.py
@@ -22,7 +22,7 @@
     return (weights.astype(jnp.float32) - learning_rate * adam_step).astype(jnp.bfloat16)
 
 
-max_levels = 1
+max_levels = 4
 
 
 def partial_products(slots, updated):
@@ -167,7 +167,7 @@
     final_half = line ^ landing_colour
     across = [(e, e ^ 1) for e in range(2 * levels)]
     local_rows, width = updated.shape[1:]
-    piece = local_rows // 2
+    piece = local_rows // 1
 
     def swap(value):
         return lax.ppermute(value, "expert", across)
@@ -183,12 +183,17 @@
         return first, second
 
     down_halves = down_local.reshape(2, width // 2, local_rows)
-    keep, send = parted(down_halves)
-    down_first, down_second = coloured(keep, swap(send))
+    kept, sent = parted(down_halves)
+    early = [coloured(kept, swap(sent))]
     proj_parts = [
-        parted(updated[:, i * piece : (i + 1) * piece]) for i in range(2)
-    ]
-    partials = partial_products(slots, updated)
+        parted(updated[:, i * piece : (i + 1) * piece]) for i in range(1)
+    ]
+    outside = 1
+    early += [coloured(keep, swap(send)) for keep, send in proj_parts[:outside]]
+    late = proj_parts[outside:]
+    returned = experts(partial_products(slots, updated))
+    firsts = [first for first, second in early]
+    seconds = [second for first, second in early]
 
     def along(perm):
         pairs = [(2 * z + x, 2 * to + x) for z, to in enumerate(perm) for x in (0, 1)]
@@ -197,49 +202,46 @@
     def first_stage(perm):
         move = along(perm)
 
-        def run(down_first, proj_parts, partials):
-            moved_down = move(down_first)
-            moved, waiting = [], []
-            for keep, send in proj_parts:
+        def run(firsts, late):
+            moved = [move(first) for first in firsts]
+            waiting = []
+            for keep, send in late:
                 first, second = coloured(keep, swap(send))
                 moved.append(move(first))
                 waiting.append(second)
-            return moved_down, moved, waiting, experts(partials)
+            return moved, waiting
 
         return run
+
+    def land(first, second):
+        keep = jnp.where(landing_colour == 0, first, second)
+        send = jnp.where(landing_colour == 0, second, first)
+        return keep, swap(send)
+
+    inside = 0
 
     def second_stage(perm):
         move = along(perm)
 
-        def run(items, moved):
-            landed = []
-            for first, waiting in zip(moved, items):
-                second = move(waiting)
-                keep = jnp.where(landing_colour == 0, first, second)
-                send = jnp.where(landing_colour == 0, second, first)
-                other = swap(send)
-                landed.append(
-                    (
-                        jnp.where(final_half == 0, keep, other),
-                        jnp.where(final_half == 0, other, keep),
-                    )
-                )
-            return landed
+        def run(seconds, moved):
+            arrived = [move(second) for second in seconds]
+            landed = [land(moved[i], arrived[i]) for i in range(inside)]
+            return landed, arrived[inside:]
 
         return run
 
-    moved_down, moved, waiting, returned = lax.switch(
-        picks[0], [first_stage(p) for p in perms], down_first, proj_parts, partials
-    )
-    landed = lax.switch(
-        picks[1],
-        [second_stage(p) for p in perms],
-        [down_second] + waiting,
-        [moved_down] + moved,
-    )
-    new_down = jnp.concatenate(landed[0], axis=0)
+    moved, waiting = lax.switch(picks[0], [first_stage(p) for p in perms], firsts, late)
+    landed, arrived = lax.switch(
+        picks[1], [second_stage(p) for p in perms], seconds + waiting, moved
+    )
+    landed = landed + [land(f, s) for f, s in zip(moved[inside:], arrived)]
+    halves = [
+        (jnp.where(final_half == 0, keep, other), jnp.where(final_half == 0, other, keep))
+        for keep, other in landed
+    ]
+    new_down = jnp.concatenate(halves[0], axis=0)
     new_proj = jnp.stack(
-        [jnp.concatenate([pair[h] for pair in landed[1:]], axis=0) for h in (0, 1)]
+        [jnp.concatenate([pair[h] for pair in halves[1:]], axis=0) for h in (0, 1)]
     )
     return new_proj, new_down, returned
 

time: 291 us -> 244 us (0.84)
  waiting for transfers between devices: 199 us -> 151 us
  other arithmetic: 14.8 us -> 36.8 us
  blocking collectives: 30.9 us -> 10.3 us
  local copies, waits for them, and re-layouts: 16.2 us -> 2.88 us
  between operations: 0.76 us -> 6.72 us
  starting transfers between devices: 23.1 us -> 29 us
    all_to_all x5 -> x2, waiting for transfers between devices: 199 us -> 43.4 us  [owner_exchange(): lax.all_to_all(pieces, 'expert', split_axis=1, concat_axis=1, tiled=True)]
    ppermute x0 -> x8, waiting for transfers between devices: none -> 105 us  [the longest x4 96.5 us: along(): return lambda value: lax.ppermute(value, 'expert', pairs)]
    all_to_all x2 -> x0, blocking collectives: 25.2 us -> none  [the longest x1 15.2 us: owner_exchange(): lax.all_to_all(pieces, 'expert', split_axis=1, concat_axis=1, tiled=True)]
    ppermute x0 -> x8, starting transfers between devices: none -> 13.3 us  [the longest x4 9.05 us: along(): return lambda value: lax.ppermute(value, 'expert', pairs)]
    all_to_all x5 -> x2, starting transfers between devices: 23.1 us -> 10.7 us  [owner_exchange(): lax.all_to_all(pieces, 'expert', split_axis=1, concat_axis=1, tiled=True)]
    select_n x3 -> x9, other arithmetic: 4.8 us -> 12.7 us  [the longest x2 4.13 us: coloured(): first = jnp.where(colour == 0, keep, other)]
    reduce_sum x1 -> x9, other arithmetic: 0.12 us -> 7.29 us  [the longest x1 1.46 us: route_choice(): jnp.sum(jnp.where(chosen[:, None] & hit, numbers[None, :], 0))]
    gather x2 -> x0, local copies, waits for them, and re-layouts: 5.83 us -> none  [the longest x1 3.2 us: two_phase_migration(): moved_down = owner_exchange(jnp.take(spread_down, inverse, axis=1))]
  transfers between devices with their start and end apart: 5 -> 11, of which waited for: 4 -> 5; matrix products, arithmetic and copies ran while one was open for 9% -> 15% of each run, Pallas kernels for 0% -> 0%
where the time goes in v2:
time: 244 us; the launch traced here: 243 us
  waiting for transfers between devices  151 us (62%)
  other arithmetic  36.8 us (15%)
  starting transfers between devices  29 us (12%)
  blocking collectives  10.3 us (4%)
  between operations  6.72 us (3%)
  matrix products  6.51 us (3%)
  local copies, waits for them, and re-layouts  2.88 us (1%)
    ppermute x4, waiting for transfers between devices, along(): return lambda value: lax.ppermute(value, 'expert', pairs)  96.5 us
    all_to_all x2, waiting for transfers between devices, owner_exchange(): lax.all_to_all(pieces, 'expert', split_axis=1, concat_axis=1, tiled=True)  43.4 us
    all_to_all x2, starting transfers between devices, owner_exchange(): lax.all_to_all(pieces, 'expert', split_axis=1, concat_axis=1, tiled=True)  10.7 us
    all_gather x1, blocking collectives, finish_rows(): lax.all_gather(hidden, 'dp', axis=0, tiled=True)  10.3 us
    ppermute x4, starting transfers between devices, along(): return lambda value: lax.ppermute(value, 'expert', pairs)  9.05 us
    convert_element_type x1, other arithmetic, adam_update(): (weights.astype(jnp.float32) - learning_rate * adam_step).astype(jnp.bflo...  9 us
    ppermute x4, waiting for transfers between devices, swap(): return lax.ppermute(value, 'expert', across)  8.86 us
    all_to_all x1, starting transfers between devices, finish_rows(): lax.all_to_all(partials.reshape(1, parts, -1, partials.shape[1]), 'dp', s...  5.1 us
  transfers between devices with their start and end apart: 11, of which 5 were waited for; matrix products, arithmetic and copies ran while one was open for 15% of the time, Pallas kernels for 0%

profile of v2, /device:TPU:0, one launch (start us, length us, event | category | flops | bytes accessed | tf_op | source)
XLA Modules:
  0.0 242.9 jit_solution(2899746931782528339)
XLA Ops:
  0.6 0.0 copy-start
  0.6 0.7 convert_reduce_fusion.1
  1.4 0.1 copy.38
  1.5 0.1 copy.40
  1.5 1.0 fusion.22
  2.6 7.3 %all-to-all-start = ((bf16[1,8,16,1024]{3,2,0,1:T(8,128)(2,1)}), bf16[1,8,16,1024]{3,2,0,1:T(8,128)(2,1)S(1)}, u32[]{:S(2)}, u32[]{:S(2)}) async-start(bf16[1,8,16,1024]{3,2,0,1:T(8,128)(2,1)} %fusion.22), calls=%async_computation | async-start | bytes 524288 | tf_op jit(solution)/shard_map/all_to_all | solution.py:54
  9.9 0.7 iota_compare_fusion.2
  10.6 0.7 fusion.44
  11.3 0.8 select_reduce_fusion
  12.1 0.8 select_reduce_fusion.5
  12.9 0.9 fusion.39
  13.7 0.6 add_reduce_fusion
  16.3 0.0 copy-start.10
  16.3 1.3 select_reduce_fusion.3
  17.7 0.7 fusion.43
  19.0 1.5 select_bitcast_fusion.2
  20.5 2.1 collective-permute-start.96
  22.6 9.0 %fusion.9 = bf16[1,2,1024,768]{3,2,1,0:T(8,128)(2,1)S(1)} fusion(f32[1,2,1024,768]{3,2,1,0:T(8,128)} %param.75, bf16[1,2,1024,768]{3,2,1,0:T(8,128)(2,1)} %param.73, f32[1,2,1024,768]{3,2,1,0:T(8,128)} %param.74, bf16[1,2,1024,768]{3,2,1,0:T(8,128)(2,1)} %param.72), kind=kLoop, calls=%fused_computation.35 | loop fusion | flops 25165824 | bytes 22020096 | tf_op jit(solution)/shard_map/convert_element_type | solution.py:22
  31.6 0.0 copy-start.4
  31.6 1.4 broadcast_select_fusion.24
  33.0 0.0 collective-permute-start.97
  33.1 0.7 copy-done.4
  33.8 1.9 slice_bitcast_fusion.1
  35.6 0.0 all-to-all-done
  35.6 3.2 %fusion.14 = bf16[128,1536]{1,0:T(8,128)(2,1)} fusion(bf16[128,1024]{1,0:T(8,128)(2,1)S(1)} %bitcast.69, bf16[1024,768]{1,0:T(8,128)(2,1)} %get-tuple-element.674, bf16[1024,768]{1,0:T(8,128)(2,1)} %get-tuple-element.673), kind=kOutput, calls=%fused_computation.41 | convolution fusion | flops 409141248 | bytes 3801088 | tf_op jit(solution)/shard_map/dot_general | solution.py:30
  38.9 5.1 %all-to-all-start.1 = ((bf16[1,4,32,1536]{3,2,0,1:T(8,128)(2,1)}), bf16[1,4,32,1536]{3,2,0,1:T(8,128)(2,1)S(1)}, u32[]{:S(2)}, u32[]{:S(2)}) async-start(bf16[1,4,32,1536]{3,2,0,1:T(8,128)(2,1)} %bitcast.68), calls=%async_computation.1 | async-start | bytes 786432 | tf_op jit(solution)/shard_map/all_to_all | solution.py:36
  44.6 1.5 fusion.40
  47.4 1.3 fusion.42
  49.4 1.9 all-to-all-done.1
  51.3 0.1 convert_reduce_fusion
  51.4 10.3 %all_gather.3 = bf16[128,768]{1,0:T(8,128)(2,1)} all-gather(bf16[32,768]{1,0:T(8,128)(2,1)S(1)} %fusion.26), channel_id=1, replica_groups=mesh['dp'=4,'expert'=8] {'dp'}, dimensions={0}, use_global_device_ids=true | all-gather | bytes 245760 | tf_op jit(solution)/shard_map/all_gather | solution.py:46
  61.7 0.0 collective-permute-done.96
  61.7 2.7 %broadcast_select_fusion.33 = (bf16[384,1024]{1,0:T(8,128)(2,1)}, bf16[384,1024]{1,0:T(8,128)(2,1)S(1)}) fusion(bf16[384,1024]{1,0:T(8,128)(2,1)S(1)} %collective-permute-done.96, pred[]{:T(512)} %eq.142, bf16[1,768,1024]{2,1,0:T(8,128)(2,1)} %param.76, pred[]{:T(512)S(6)} %eq.143), kind=kLoop, calls=%fused_computation.67 | loop fusion | flops 786432 | bytes 3932162 | tf_op jit(solution)/shard_map/jit(_where)/select_n | solution.py:181
  64.4 8.8 %collective-permute-done.97 = bf16[1024,768]{1,0:T(8,128)(2,1)S(1)} collective-permute-done((bf16[1024,768]{1,0:T(8,128)(2,1)}, bf16[1024,768]{1,0:T(8,128)(2,1)S(1)}, u32[]{:S(2)}, u32[]{:S(2)}) %collective-permute-start.97) | collective-permute-done | bytes 1572896 | tf_op jit(solution)/shard_map/ppermute | solution.py:173
  73.3 1.4 broadcast_select_fusion.26
  74.7 0.1 select_n.377
  74.8 54.9 %conditional.3 = (bf16[384,1024]{1,0:T(8,128)(2,1)}, bf16[1024,768]{1,0:T(8,128)(2,1)}) conditional(s32[]{:T(128)} %clamp.7, (pred[384,1024]{1,0:T(8,128)(4,1)S(1)}, bf16[384,1024]{1,0:T(8,128)(2,1)S(1)}, bf16[384,1024]{1,0:T(8,128)(2,1)S(1)}, pred[]{:T(512)}, bf16[1024,768]{1,0:T(8,128)(2,1)S(1)}, ...), branch_computations={%region_42.43_spmd, %region_43.44_spmd, %region_44.45_spmd, %regio... | conditional | flops 1179648 | bytes 16908384 | solution.py:234
  74.8 0.2 broadcast_select_fusion.8
  75.0 3.6 %collective-permute-start.65 = (bf16[1024,768]{1,0:T(8,128)(2,1)S(1)}, bf16[1024,768]{1,0:T(8,128)(2,1)}, u32[]{:S(2)}, u32[]{:S(2)}) collective-permute-start(bf16[1024,768]{1,0:T(8,128)(2,1)S(1)} %broadcast_select_fusion.8), channel_id=1, source_target_pairs={{0,2},{1,3},{2,4},{3,5},{4,0},{5,1},{6,6},{7,7},{8,10},{9,11},{10,... | collective-permute-start | bytes 4718600 | tf_op jit(solution)/shard_map/cond/branch_8_fun/ppermute | solution.py:200
  78.7 0.3 select_n.274
  79.0 3.4 %collective-permute-start.64 = (bf16[384,1024]{1,0:T(8,128)(2,1)S(1)}, bf16[384,1024]{1,0:T(8,128)(2,1)}, u32[]{:S(2)}, u32[]{:S(2)}) collective-permute-start(bf16[384,1024]{1,0:T(8,128)(2,1)S(1)} %select_n.274), channel_id=1, source_target_pairs={{0,2},{1,3},{2,4},{3,5},{4,0},{5,1},{6,6},{7,7},{8,10},{9,11},{10,... | collective-permute-start | bytes 2359304 | tf_op jit(solution)/shard_map/cond/branch_8_fun/ppermute | solution.py:200
  82.4 47.3 %collective-permute-done.64 = bf16[384,1024]{1,0:T(8,128)(2,1)} collective-permute-done((bf16[384,1024]{1,0:T(8,128)(2,1)S(1)}, bf16[384,1024]{1,0:T(8,128)(2,1)}, u32[]{:S(2)}, u32[]{:S(2)}) %collective-permute-start.64) | collective-permute-done | bytes 786464 | tf_op jit(solution)/shard_map/cond/branch_8_fun/ppermute | solution.py:200
  129.7 0.0 collective-permute-done.65
  129.7 51.2 %conditional.2 = (bf16[384,1024]{1,0:T(8,128)(2,1)}, bf16[1024,768]{1,0:T(8,128)(2,1)}) conditional(s32[]{:T(128)} %clamp.6, (bf16[384,1024]{1,0:T(8,128)(2,1)}, bf16[1024,768]{1,0:T(8,128)(2,1)}) %tuple.200, (bf16[384,1024]{1,0:T(8,128)(2,1)}, bf16[1024,768]{1,0:T(8,128)(2,1)}) %tuple.200, ...), branch_computations={%region_17.18_spmd, %region_18.19_spmd, %region_19.20_spmd, %regio... | conditional | bytes 9437280 | solution.py:233
  129.7 0.5 collective-permute-start.15
  130.3 1.5 collective-permute-start.14
  131.7 49.2 %collective-permute-done.14 = bf16[384,1024]{1,0:T(8,128)(2,1)} collective-permute-done((bf16[384,1024]{1,0:T(8,128)(2,1)}, bf16[384,1024]{1,0:T(8,128)(2,1)}, u32[]{:S(2)}, u32[]{:S(2)}) %collective-permute-start.14) | collective-permute-done | bytes 786464 | tf_op jit(solution)/shard_map/cond/branch_7_fun/ppermute | solution.py:200
  180.9 0.0 collective-permute-done.15
  180.9 1.6 broadcast_select_fusion.27
  182.5 0.0 copy-start.6
  182.5 1.2 collective-permute-start.98
  183.7 2.1 broadcast_select_fusion.29
  185.8 0.9 collective-permute-start.99
  186.7 1.1 fusion.19
  187.8 3.4 %all-to-all-start.2 = ((bf16[1,8,16,1024]{3,2,0,1:T(8,128)(2,1)}), bf16[1,8,16,1024]{3,2,0,1:T(8,128)(2,1)S(1)}, u32[]{:S(2)}, u32[]{:S(2)}) async-start(bf16[1,8,16,1024]{3,2,0,1:T(8,128)(2,1)} %bitcast.16), calls=%async_computation.2 | async-start | bytes 524288 | tf_op jit(solution)/shard_map/all_to_all | solution.py:54
  191.9 43.4 %all-to-all-done.2 = bf16[1,8,16,1024]{3,2,0,1:T(8,128)(2,1)S(1)} async-done(((bf16[1,8,16,1024]{3,2,0,1:T(8,128)(2,1)}), bf16[1,8,16,1024]{3,2,0,1:T(8,128)(2,1)S(1)}, u32[]{:S(2)}, u32[]{:S(2)}) %all-to-all-start.2) | async-done | bytes 262176 | tf_op jit(solution)/shard_map/all_to_all | solution.py:54
  235.3 1.1 fusion.24
  236.5 0.0 collective-permute-done.99
  236.5 1.5 broadcast_select_fusion.32
  238.0 1.3 maximum_bitcast_fusion.1
  239.3 0.0 collective-permute-done.98
  239.3 1.7 select_bitcast_fusion.1
  241.0 0.0 copy-start.1
  241.0 1.9 maximum_bitcast_fusion
  (24 shorter events, 0.2 us)
Async XLA Ops:
  0.6 0.9 copy-start
  2.6 33.0 %all-to-all-start = ((bf16[1,8,16,1024]{3,2,0,1:T(8,128)(2,1)}), bf16[1,8,16,1024]{3,2,0,1:T(8,128)(2,1)S(1)}, u32[]{:S(2)}, u32[]{:S(2)}) async-start(bf16[1,8,16,1024]{3,2,0,1:T(8,128)(2,1)} %fusion.22), calls=%async_computation | async-start | bytes 524288 | tf_op jit(solution)/shard_map/all_to_all | solution.py:54
  16.3 15.3 %copy-start.10 = (pred[16]{0:T(512)(128)(4,1)}, pred[16]{0:T(512)(128)(4,1)S(1)}, u32[]{:S(2)}) copy-start(pred[16]{0:T(512)(128)(4,1)S(1)} %iota_compare_fusion.3) | copy-start | bytes 52
  20.5 41.2 %collective-permute-start.96 = (bf16[384,1024]{1,0:T(8,128)(2,1)S(1)}, bf16[384,1024]{1,0:T(8,128)(2,1)S(1)}, u32[]{:S(2)}, u32[]{:S(2)}) collective-permute-start(bf16[384,1024]{1,0:T(8,128)(2,1)S(1)} %select_bitcast_fusion.2), channel_id=1, source_target_pairs={{0,1},{1,0},{2,3},{3,2},{4,5},{5,4},{6,7},{7,6},{8,9},{9,8},{10,11... | collective-permute-start | bytes 2359304 | tf_op jit(solution)/shard_map/ppermute | solution.py:173
  31.6 2.2 copy-start.4
  33.0 40.2 %collective-permute-start.97 = (bf16[1024,768]{1,0:T(8,128)(2,1)}, bf16[1024,768]{1,0:T(8,128)(2,1)S(1)}, u32[]{:S(2)}, u32[]{:S(2)}) collective-permute-start(bf16[1024,768]{1,0:T(8,128)(2,1)} %broadcast_select_fusion.24), channel_id=1, source_target_pairs={{0,1},{1,0},{2,3},{3,2},{4,5},{5,4},{6,7},{7,6},{8,9},{9,8},{10,11... | collective-permute-start | bytes 4718600 | tf_op jit(solution)/shard_map/ppermute | solution.py:173
  38.9 12.4 %all-to-all-start.1 = ((bf16[1,4,32,1536]{3,2,0,1:T(8,128)(2,1)}), bf16[1,4,32,1536]{3,2,0,1:T(8,128)(2,1)S(1)}, u32[]{:S(2)}, u32[]{:S(2)}) async-start(bf16[1,4,32,1536]{3,2,0,1:T(8,128)(2,1)} %bitcast.68), calls=%async_computation.1 | async-start | bytes 786432 | tf_op jit(solution)/shard_map/all_to_all | solution.py:36
  61.7 11.6 %copy-start.5 = (bf16[1,2,1024,768]{3,2,1,0:T(8,128)(2,1)S(1)}, bf16[1,2,1024,768]{3,2,1,0:T(8,128)(2,1)}, u32[]{:S(2)}) copy-start(bf16[1,2,1024,768]{3,2,1,0:T(8,128)(2,1)} %copy-done.4) | copy-start | bytes 9437188
  61.7 2.7 %copy-start.2 = (bf16[384,1024]{1,0:T(8,128)(2,1)}, bf16[384,1024]{1,0:T(8,128)(2,1)S(1)}, u32[]{:S(2)}) copy-start(bf16[384,1024]{1,0:T(8,128)(2,1)S(1)} %collective-permute-done.96) | copy-start | bytes 2359300
  73.3 1.5 copy-start.3
  75.0 54.7 %collective-permute-start.65 = (bf16[1024,768]{1,0:T(8,128)(2,1)S(1)}, bf16[1024,768]{1,0:T(8,128)(2,1)}, u32[]{:S(2)}, u32[]{:S(2)}) collective-permute-start(bf16[1024,768]{1,0:T(8,128)(2,1)S(1)} %broadcast_select_fusion.8), channel_id=1, source_target_pairs={{0,2},{1,3},{2,4},{3,5},{4,0},{5,1},{6,6},{7,7},{8,10},{9,11},{10,... | collective-permute-start | bytes 4718600 | tf_op jit(solution)/shard_map/cond/branch_8_fun/ppermute | solution.py:200
  79.0 50.7 %collective-permute-start.64 = (bf16[384,1024]{1,0:T(8,128)(2,1)S(1)}, bf16[384,1024]{1,0:T(8,128)(2,1)}, u32[]{:S(2)}, u32[]{:S(2)}) collective-permute-start(bf16[384,1024]{1,0:T(8,128)(2,1)S(1)} %select_n.274), channel_id=1, source_target_pairs={{0,2},{1,3},{2,4},{3,5},{4,0},{5,1},{6,6},{7,7},{8,10},{9,11},{10,... | collective-permute-start | bytes 2359304 | tf_op jit(solution)/shard_map/cond/branch_8_fun/ppermute | solution.py:200
  129.7 51.2 %collective-permute-start.15 = (bf16[1024,768]{1,0:T(8,128)(2,1)}, bf16[1024,768]{1,0:T(8,128)(2,1)}, u32[]{:S(2)}, u32[]{:S(2)}) collective-permute-start(bf16[1024,768]{1,0:T(8,128)(2,1)} %get-tuple-element.471), channel_id=1, source_target_pairs={{0,2},{1,3},{2,0},{3,1},{4,6},{5,7},{6,4},{7,5},{8,10},{9,11},{10,... | collective-permute-start | bytes 4718600 | tf_op jit(solution)/shard_map/cond/branch_7_fun/ppermute | solution.py:200
  130.3 50.6 %collective-permute-start.14 = (bf16[384,1024]{1,0:T(8,128)(2,1)}, bf16[384,1024]{1,0:T(8,128)(2,1)}, u32[]{:S(2)}, u32[]{:S(2)}) collective-permute-start(bf16[384,1024]{1,0:T(8,128)(2,1)} %get-tuple-element.470), channel_id=1, source_target_pairs={{0,2},{1,3},{2,0},{3,1},{4,6},{5,7},{6,4},{7,5},{8,10},{9,11},{10,... | collective-permute-start | bytes 2359304 | tf_op jit(solution)/shard_map/cond/branch_7_fun/ppermute | solution.py:200
  182.5 4.2 %copy-start.6 = (bf16[1,768,1024]{2,1,0:T(8,128)(2,1)S(1)}, bf16[1,768,1024]{2,1,0:T(8,128)(2,1)}, u32[]{:S(2)}) copy-start(bf16[1,768,1024]{2,1,0:T(8,128)(2,1)} %param.76) | copy-start | bytes 4718596
  182.5 4.2 %copy-start.7 = (bf16[128,768]{1,0:T(8,128)(2,1)S(1)}, bf16[128,768]{1,0:T(8,128)(2,1)}, u32[]{:S(2)}) copy-start(bf16[128,768]{1,0:T(8,128)(2,1)} %all_gather.3) | copy-start | bytes 589828
  182.5 56.8 %collective-permute-start.98 = (bf16[1024,768]{1,0:T(8,128)(2,1)S(1)}, bf16[1024,768]{1,0:T(8,128)(2,1)S(1)}, u32[]{:S(2)}, u32[]{:S(2)}) collective-permute-start(bf16[1024,768]{1,0:T(8,128)(2,1)S(1)} %broadcast_select_fusion.27), channel_id=1, source_target_pairs={{0,1},{1,0},{2,3},{3,2},{4,5},{5,4},{6,7},{7,6},{8,9},{9,8},{10,11... | collective-permute-start | bytes 4718600 | tf_op jit(solution)/shard_map/ppermute | solution.py:173
  185.8 6.1 %copy-start.8 = (s32[1,16,8]{1,2,0:T(8,128)S(1)}, s32[1,16,8]{1,2,0:T(8,128)}, u32[]{:S(2)}) copy-start(s32[1,16,8]{1,2,0:T(8,128)} %param.69) | copy-start | bytes 1540
  185.8 6.1 %copy-start.9 = (f32[1,16,8]{1,2,0:T(8,128)S(1)}, f32[1,16,8]{1,2,0:T(8,128)}, u32[]{:S(2)}) copy-start(f32[1,16,8]{1,2,0:T(8,128)} %param.70) | copy-start | bytes 1540
  185.8 50.7 %collective-permute-start.99 = (bf16[384,1024]{1,0:T(8,128)(2,1)}, bf16[384,1024]{1,0:T(8,128)(2,1)}, u32[]{:S(2)}, u32[]{:S(2)}) collective-permute-start(bf16[384,1024]{1,0:T(8,128)(2,1)} %broadcast_select_fusion.29), channel_id=1, source_target_pairs={{0,1},{1,0},{2,3},{3,2},{4,5},{5,4},{6,7},{7,6},{8,9},{9,8},{10,11... | collective-permute-start | bytes 2359304 | tf_op jit(solution)/shard_map/ppermute | solution.py:173
  187.8 47.5 %all-to-all-start.2 = ((bf16[1,8,16,1024]{3,2,0,1:T(8,128)(2,1)}), bf16[1,8,16,1024]{3,2,0,1:T(8,128)(2,1)S(1)}, u32[]{:S(2)}, u32[]{:S(2)}) async-start(bf16[1,8,16,1024]{3,2,0,1:T(8,128)(2,1)} %bitcast.16), calls=%async_computation.2 | async-start | bytes 524288 | tf_op jit(solution)/shard_map/all_to_all | solution.py:54
  241.0 2.0 copy-start.1
